TPU v7x, 32 devices: a whole 2x2x4 slice. The times are simulated.
32 devices in a mesh: groups: 2 (over x), segment: 4 (over y, core), head: 4 (over z).
Axes of the slice: x: 2, y: 2, z: 4, core: 2. Of those that a mesh axis runs over, the one named last changes fastest.
Arguments:
- token_ids: int32 [6, 256], P('groups'), parts along dimension 0, may hold values from 0 to 18991, as said below
- embed_table: bfloat16 [18992, 256], P(('segment', 'head')), may hold values from -6 to 6
- arriving: bfloat16 [8, 256, 256], P(('groups', 'segment')), parts along dimension 0, may hold values from -16 to 16
- returning: bfloat16 [8, 256, 256], P(('groups', 'segment')), parts along dimension 0, may hold values from -6 to 6
- stashed: bfloat16 [8, 3, 256, 256], P(('groups', 'segment')), parts along dimension 0, may hold values from -16 to 16
- seed_grad: bfloat16 [6, 256, 256], P('groups'), parts along dimension 0, may hold values from -6 to 6
- expand: bfloat16 [4, 256, 2048], P('segment'), may hold values from -0.375 to 0.375
- compress: bfloat16 [4, 2048, 256], P('segment'), may hold values from -0.125 to 0.125
- norm_gain: float32 [4, 2048], P('segment'), may hold values from 0.1 to 1.9
- w_query: bfloat16 [4, 2048, 4096], P('segment', None, 'head'), may hold values from -0.125 to 0.125
- key_weight: bfloat16 [4, 2048, 512], P('segment'), may hold values from -0.125 to 0.125
- value_weight: bfloat16 [4, 2048, 512], P('segment'), may hold values from -0.125 to 0.125
- w_out: bfloat16 [4, 4096, 2048], P('segment', 'head'), may hold values from -0.09375 to 0.09375
Outputs:
- sent_forward: bfloat16 [8, 3, 256, 256], P(('groups', 'segment'), None, 'head'), parts along dimension 0
- sent_backward: bfloat16 [8, 3, 256, 256], P(('groups', 'segment'), None, 'head'), parts along dimension 0
There are 2 independent parts, one for each index of `groups`. A program takes and returns all parts, laid end to end along the dimension named above; an argument that names none is the same for every part. Nothing has to cross between parts.
Inputs may be any that keep to these rules, and one draw needn't show every extreme that they name: `token_ids`: every aligned block of 1187 ids is named by some token.
All inputs are finite; a program needn't handle non-finite values.
Results may differ from a plain program's by a relative error of at most 0.02.
Values may be sent and summed in bfloat16 or wider, within the bound.
A program may use at most 128 MiB of HBM per device.

v0:
```python
import math
import jax
import jax.numpy as jnp
from jax import lax
from jax.sharding import PartitionSpec as P

QUERY_HEADS = 32
KEY_VALUE_HEADS = 4
HEAD_SIZE = 128
EPS = 1e-06


def passed_along(x, axis, by):
    length = lax.axis_size(axis)
    pairs = [(i, i + by) for i in range(length) if 0 <= i + by < length]
    return lax.ppermute(x, axis, pairs)


def rms_scale(matrix):
    return lax.rsqrt(jnp.mean(matrix * matrix, axis=-1, keepdims=True) + EPS)


def precise(former, latter):
    return jnp.dot(
        former, latter, precision=lax.Precision.HIGHEST, preferred_element_type=jnp.float32
    )


def precise_back(former, latter):
    return lax.dot_general(
        former,
        latter,
        (((1,), (1,)), ((), ())),
        precision=lax.Precision.HIGHEST,
        preferred_element_type=jnp.float32,
    )


def narrow_back(former, latter):
    return lax.dot_general(
        former, latter, (((1,), (1,)), ((), ())), preferred_element_type=jnp.float32
    )


def norm_back(upstream_in, grad_hat):
    scaling = rms_scale(upstream_in)
    return scaling * grad_hat - upstream_in * scaling**3 * jnp.mean(
        grad_hat * upstream_in, axis=-1, keepdims=True
    )


def section_inputs(coeffs, expand_here, gain_here, query_here, key_here, value_here):
    row_count = coeffs.shape[0]
    hidden = jnp.dot(coeffs, expand_here, preferred_element_type=jnp.float32)
    scaling = rms_scale(hidden)
    normed = (hidden * scaling * gain_here).astype(jnp.bfloat16)
    queries = jnp.dot(normed, query_here, preferred_element_type=jnp.float32).reshape(
        row_count, -1, HEAD_SIZE
    )
    key_rows = jnp.dot(normed, key_here, preferred_element_type=jnp.float32).reshape(
        row_count, -1, HEAD_SIZE
    )
    values = (
        jnp.dot(normed, value_here, preferred_element_type=jnp.float32)
        .astype(jnp.bfloat16)
        .reshape(row_count, -1, HEAD_SIZE)
    )
    q_hat = (queries * rms_scale(queries)).astype(jnp.bfloat16)
    k_hat = (key_rows * rms_scale(key_rows)).astype(jnp.bfloat16)
    return (hidden, scaling, queries, key_rows, q_hat, k_hat, values)


def probabilities(q_hat, k_hat):
    row_count, head_count, head_width = q_hat.shape
    kv_heads = k_hat.shape[1]
    grouped = q_hat.reshape(row_count, kv_heads, head_count // kv_heads, head_width)
    scores = jnp.einsum(
        "iknd,jkd->knij", grouped, k_hat, preferred_element_type=jnp.float32
    ) / math.sqrt(head_width)
    causal = jnp.arange(row_count)[None, :] <= jnp.arange(row_count)[:, None]
    weights = jnp.where(causal, jnp.exp(scores), 0.0)
    return weights / jnp.sum(weights, axis=-1, keepdims=True)


def section_forward(coeffs, expand_here, gain_here, query_here, key_here, value_here, out_folded):
    hidden, scaling, queries, key_rows, q_hat, k_hat, values = section_inputs(
        coeffs, expand_here, gain_here, query_here, key_here, value_here
    )
    weights = probabilities(q_hat, k_hat)
    attended = jnp.einsum(
        "knij,jkd->iknd", weights.astype(jnp.bfloat16), values, preferred_element_type=jnp.float32
    )
    attended = attended.reshape(coeffs.shape[0], -1).astype(jnp.bfloat16)
    return jnp.dot(attended, out_folded, preferred_element_type=jnp.float32)


def section_backward(
    coeffs, grads, expand_here, gain_here, query_here, key_here, value_here, out_folded
):
    row_count = coeffs.shape[0]
    hidden, scaling, queries, key_rows, q_hat, k_hat, values = section_inputs(
        coeffs, expand_here, gain_here, query_here, key_here, value_here
    )
    weights = probabilities(q_hat, k_hat)
    head_count = queries.shape[1]
    kv_heads = key_rows.shape[1]
    query_group_size = head_count // kv_heads
    grad_attended = narrow_back(grads, out_folded).astype(jnp.bfloat16)
    grad_attended = grad_attended.reshape(row_count, kv_heads, query_group_size, HEAD_SIZE)
    grad_weights = jnp.einsum(
        "iknd,jkd->knij", grad_attended, values, preferred_element_type=jnp.float32
    )
    grad_scores = (
        weights
        * (grad_weights - jnp.sum(grad_weights * weights, axis=-1, keepdims=True))
        / math.sqrt(HEAD_SIZE)
    )
    grad_scores = grad_scores.astype(jnp.bfloat16)
    grouped = q_hat.reshape(row_count, kv_heads, query_group_size, HEAD_SIZE)
    grad_qhat = jnp.einsum(
        "knij,jkd->iknd", grad_scores, k_hat, preferred_element_type=jnp.float32
    ).reshape(row_count, head_count, HEAD_SIZE)
    grad_khat = jnp.einsum(
        "knij,iknd->jkd", grad_scores, grouped, preferred_element_type=jnp.float32
    )
    grad_values = jnp.einsum(
        "knij,iknd->jkd",
        weights.astype(jnp.bfloat16),
        grad_attended,
        preferred_element_type=jnp.float32,
    )
    grad_values = grad_values.reshape(row_count, -1).astype(jnp.bfloat16)
    grad_queries = norm_back(queries, grad_qhat).reshape(row_count, -1).astype(jnp.bfloat16)
    grad_keys = norm_back(key_rows, grad_khat).reshape(row_count, -1).astype(jnp.bfloat16)
    grad_normed = (
        narrow_back(grad_queries, query_here)
        + narrow_back(grad_keys, key_here)
        + narrow_back(grad_values, value_here)
    )
    weighted = grad_normed * gain_here
    grad_hidden = scaling * weighted - hidden * scaling**3 * jnp.mean(
        weighted * hidden, axis=-1, keepdims=True
    )
    return narrow_back(grad_hidden.astype(jnp.bfloat16), expand_here)


def shards(
    token_ids,
    embed_table,
    arriving,
    returning,
    stashed,
    seed_grad,
    expand,
    compress,
    norm_gain,
    w_query,
    key_weight,
    value_weight,
    w_out,
):
    segment_index = lax.axis_index("segment")
    last_segment = lax.axis_size("segment") - 1
    head_index = lax.axis_index("head")
    heads_here = w_query.shape[2] // HEAD_SIZE
    query_group_size = QUERY_HEADS // KEY_VALUE_HEADS
    kv_here = (heads_here + query_group_size - 1) // query_group_size
    first_kv = head_index * heads_here // query_group_size
    expand_here = expand[0]
    gain_here = norm_gain[0]
    query_here = w_query[0]
    key_here = lax.dynamic_slice_in_dim(key_weight[0], first_kv * HEAD_SIZE, kv_here * HEAD_SIZE, 1)
    value_here = lax.dynamic_slice_in_dim(
        value_weight[0], first_kv * HEAD_SIZE, kv_here * HEAD_SIZE, 1
    )
    basis_folded = jnp.dot(expand_here, compress[0], preferred_element_type=jnp.float32)
    out_folded = jnp.dot(w_out[0], compress[0], preferred_element_type=jnp.float32).astype(
        jnp.bfloat16
    )
    table_rows = embed_table.shape[0]
    local_ids = token_ids.reshape(-1) - lax.axis_index(("segment", "head")) * table_rows
    inside = (local_ids >= 0) & (local_ids < table_rows)
    looked = jnp.take(embed_table, jnp.clip(local_ids, 0, table_rows - 1), axis=0).astype(
        jnp.float32
    )
    picked = jnp.where(inside[:, None], looked, 0.0)
    embedded = lax.psum(picked, ("segment", "head")).astype(jnp.bfloat16)
    tick_count = token_ids.shape[0]
    span_rows = token_ids.shape[1]
    embedded = embedded.reshape(tick_count, span_rows, -1)
    share_rows = span_rows // lax.axis_size("head")
    share_start = head_index * share_rows
    forward_recv = arriving[0]
    backward_recv = returning[0]
    history = []
    forward_shares = []
    backward_shares = []
    for tick_index in range(tick_count):
        more_ticks = tick_index + 1 < tick_count
        forward_in = jnp.where(segment_index == 0, embedded[tick_index], forward_recv)
        backward_in = jnp.where(segment_index == last_segment, seed_grad[tick_index], backward_recv)
        history.append(forward_in)
        delay_ticks = 2 * (last_segment - segment_index)
        replay = stashed[0, tick_index]
        for earlier in range(tick_index + 1):
            replay = jnp.where(delay_ticks == tick_index - earlier, history[earlier], replay)
        partial_value = section_forward(
            forward_in, expand_here, gain_here, query_here, key_here, value_here, out_folded
        )
        direct = precise(forward_in.astype(jnp.float32), basis_folded)
        summed = lax.psum_scatter(
            partial_value.astype(jnp.bfloat16), "head", scatter_dimension=0, tiled=True
        ).astype(jnp.float32)
        own_rows = (summed + lax.dynamic_slice_in_dim(direct, share_start, share_rows, 0)).astype(
            jnp.bfloat16
        )
        forward_shares.append(own_rows)
        if more_ticks:
            arrived = passed_along(own_rows, "segment", 1)
            forward_recv = lax.all_gather(arrived, "head", axis=0, tiled=True)
        partial_back = section_backward(
            replay,
            backward_in,
            expand_here,
            gain_here,
            query_here,
            key_here,
            value_here,
            out_folded,
        )
        direct_back = precise_back(backward_in.astype(jnp.float32), basis_folded)
        summed_back = lax.psum_scatter(
            partial_back.astype(jnp.bfloat16), "head", scatter_dimension=0, tiled=True
        ).astype(jnp.float32)
        own_back = (
            summed_back + lax.dynamic_slice_in_dim(direct_back, share_start, share_rows, 0)
        ).astype(jnp.bfloat16)
        backward_shares.append(own_back)
        if more_ticks:
            arrived_back = passed_along(own_back, "segment", -1)
            backward_recv = lax.all_gather(arrived_back, "head", axis=0, tiled=True)
    sent_forward = jnp.stack(forward_shares)[None]
    sent_backward = jnp.stack(backward_shares)[None]
    return (sent_forward, sent_backward)


def solution(mesh):
    return jax.shard_map(
        shards,
        mesh=mesh,
        in_specs=(
            P("groups", None),
            P(("segment", "head"), None),
            P(("groups", "segment"), None, None),
            P(("groups", "segment"), None, None),
            P(("groups", "segment"), None, None, None),
            P("groups", None, None),
            P("segment", None, None),
            P("segment", None, None),
            P("segment", None),
            P("segment", None, "head"),
            P("segment", None, None),
            P("segment", None, None),
            P("segment", "head", None),
        ),
        out_specs=(
            P(("groups", "segment"), None, "head", None),
            P(("groups", "segment"), None, "head", None),
        ),
        check_vma=False,
    )
```

profile of v0, /device:TPU:0, one launch (start us, length us, event | category | flops | bytes accessed | tf_op | source)
XLA Modules:
  0.0 454.7 jit_solution(9600917615611538147)
XLA Ops:
  9.6 4.0 gather_fusion
  13.6 2.3 convert_select_fusion
  15.9 78.0 %all-reduce.1 = bf16[768,256]{1,0:T(8,128)(2,1)} all-reduce(f32[768,256]{1,0:T(8,128)} %convert_select_fusion), channel_id=1, replica_groups=mesh['groups'=2,'segment'=4,'head'=4] {'segment','head'}, use_global_device_ids=true, to_apply=%region_0.1 | all-reduce | flops 196608 | bytes 1179648 | tf_op jit(solution)/shard_map/psum | solution.py:187
  96.7 1.8 multiply_convert_fusion.5
  101.1 6.5 %copy.87 = bf16[1024,2048]{1,0:T(8,128)(2,1)} copy(bf16[1024,2048]{0,1:T(8,128)(2,1)} %bitcast.659) | data formatting | bytes 8388608 | tf_op jit(solution)/shard_map/dot_general | solution.py:57
  107.6 4.0 multiply_reduce_fusion.17
  111.7 2.0 fusion.32
  113.7 1.9 fusion.23
  115.7 3.7 convolution_convert_fusion.5
  119.4 2.2 convolution_convert_fusion.8
  123.4 2.7 multiply_reduce_fusion.5
  126.1 1.9 fusion.155
  129.0 2.3 convolution_convert_fusion.2
  131.3 9.0 %reduce-scatter.7.cloned.1.call-done = bf16[64,256]{1,0:T(8,128)(2,1)} async-done(((bf16[256,256]{1,0:T(8,128)(2,1)}), bf16[64,256]{1,0:T(8,128)(2,1)}) %reduce-scatter.7.cloned.1.call-update) | async-done | bytes 32784 | tf_op jit(solution)/shard_map/reduce_scatter | solution.py:211
  141.8 1.9 collective-permute-start
  144.2 2.0 copy.92
  146.1 13.8 %all_gather.12 = bf16[256,256]{1,0:T(8,128)(2,1)S(1)} all-gather(bf16[64,256]{1,0:T(8,128)(2,1)} %collective-permute-done), channel_id=1, replica_groups=mesh['groups'=2,'segment'=4,'head'=4] {'head'}, dimensions={0}, use_global_device_ids=true | all-gather | bytes 163840 | tf_op jit(solution)/shard_map/all_gather | solution.py:220
  167.8 2.3 multiply_reduce_fusion.12
  173.0 2.9 multiply_reduce_fusion.14
  177.1 2.5 fusion.24
  179.6 3.8 convolution_convert_fusion.4
  183.4 2.2 convolution_convert_fusion.7
  187.6 3.1 fusion.141
  192.2 12.4 %reduce-scatter.9.cloned.1.call-done = bf16[64,256]{1,0:T(8,128)(2,1)} async-done(((bf16[256,256]{1,0:T(8,128)(2,1)}), bf16[64,256]{1,0:T(8,128)(2,1)}) %reduce-scatter.9.cloned.1.call-update) | async-done | bytes 32784 | tf_op jit(solution)/shard_map/reduce_scatter | solution.py:211
  208.6 13.7 %all_gather.13 = bf16[256,256]{1,0:T(8,128)(2,1)S(1)} all-gather(bf16[64,256]{1,0:T(8,128)(2,1)S(1)} %collective-permute-done.1), channel_id=1, replica_groups=mesh['groups'=2,'segment'=4,'head'=4] {'head'}, dimensions={0}, use_global_device_ids=true | all-gather | bytes 163840 | tf_op jit(solution)/shard_map/all_gather | solution.py:220
  227.3 2.3 multiply_reduce_fusion.18
  232.2 3.3 fusion.31
  235.5 5.0 %fusion.19 = (f32[8,256]{1,0:T(8,128)}, f32[256,256,8]{1,0,2:T(8,128)}) fusion(f32[8,256]{1,0:T(8,128)S(1)} %get-tuple-element.5, f32[256,256,8]{1,0,2:T(8,128)} %fusion.141, pred[256,256]{0,1:T(8,128)(4,1)S(1)} %copy-done.28, bf16[256,2048]{1,0:T(8,128)(2,1)} %copy-done.13, bf16[1,2048,512]{2,1,0:T(8,128)(2,1)S(1)} %copy-done, s32[]{:T(128)S(6)} %select_n.142, ...), kind=kOutput, calls=%fused_computation.38 | convolution fusion | flops 271087616 | bytes 6373380 | tf_op jit(solution)/shard_map/iknd,jkd->knij/dot_general | solution.py:110
  240.4 4.1 convert_bitcast_fusion.2
  246.3 1.9 multiply_reduce_fusion.13
  248.2 2.9 multiply_reduce_fusion.15
  251.1 3.0 copy.65
  257.3 3.6 fusion.4
  260.9 2.9 convolution_add_fusion.5
  263.7 5.1 %multiply_reduce_fusion.4 = (f32[256]{0:T(256)S(1)}, f32[256,2048]{1,0:T(8,128)}) fusion(f32[256,2048]{1,0:T(8,128)} %get-tuple-element.49, f32[2048]{0:T(1024)S(1)} %bitcast.678, f32[256,2048]{1,0:T(8,128)} %convolution_add_fusion.5, bf16[1,2048,512]{2,1,0:T(8,128)(2,1)S(1)} %copy-done, s32[]{:T(128)S(6)} %select_n.142, ...), kind=kOutput, calls=%fused_computation.51 | convolution fusion | flops 270565120 | bytes 8397828 | tf_op jit(solution)/shard_map/dot_general | solution.py:40
  268.8 3.5 convolution_convert_fusion.11
  273.0 3.1 multiply_reduce_fusion.21
  276.1 16.2 %reduce-scatter.13.cloned.1.call-done = bf16[64,256]{1,0:T(8,128)(2,1)} async-done(((bf16[256,256]{1,0:T(8,128)(2,1)}), bf16[64,256]{1,0:T(8,128)(2,1)}) %reduce-scatter.13.cloned.1.call-update) | async-done | bytes 32784 | tf_op jit(solution)/shard_map/reduce_scatter | solution.py:232
  296.2 13.5 %all_gather.14 = bf16[256,256]{1,0:T(8,128)(2,1)S(1)} all-gather(bf16[64,256]{1,0:T(8,128)(2,1)S(1)} %collective-permute-done.2), channel_id=1, replica_groups=mesh['groups'=2,'segment'=4,'head'=4] {'head'}, dimensions={0}, use_global_device_ids=true | all-gather | bytes 163840 | tf_op jit(solution)/shard_map/all_gather | solution.py:241
  310.4 2.2 convolution_convert_fusion.1
  312.6 5.0 %fusion.15 = (f32[8,256]{1,0:T(8,128)}, f32[256,256,8]{1,0,2:T(8,128)}) fusion(f32[8,256]{1,0:T(8,128)} %get-tuple-element.6, f32[256,256,8]{1,0,2:T(8,128)} %copy-done.10, pred[256,256]{0,1:T(8,128)(4,1)S(1)} %copy-done.29, bf16[256,2048]{1,0:T(8,128)(2,1)} %copy-done.12, bf16[1,2048,512]{2,1,0:T(8,128)(2,1)S(1)} %copy-done, s32[]{:T(128)S(6)} %select_n.142, ...), kind=kOutput, calls=%fused_computation.32 | convolution fusion | flops 271087616 | bytes 6373380 | tf_op jit(solution)/shard_map/iknd,jkd->knij/dot_general | solution.py:110
  317.6 4.0 convert_bitcast_fusion.1
  323.3 1.9 multiply_reduce_fusion.11
  326.1 2.6 copy.71
  331.9 3.6 fusion.2
  335.5 2.9 convolution_add_fusion.3
  338.3 5.1 %multiply_reduce_fusion.2 = (f32[256]{0:T(256)S(1)}, f32[256,2048]{1,0:T(8,128)}) fusion(f32[256,2048]{1,0:T(8,128)} %copy-done.3, f32[2048]{0:T(1024)S(1)} %bitcast.679, f32[256,2048]{1,0:T(8,128)} %convolution_add_fusion.3, bf16[1,2048,512]{2,1,0:T(8,128)(2,1)S(1)} %copy-done, s32[]{:T(128)S(6)} %select_n.142, bf16[256,8,128]{2,1,0:T(8,128)(2,1)} %bitcast.671, ...), kind=kOutput, calls=%fused_computation.47 | convolution fusion | flops 270565120 | bytes 8397828 | tf_op jit(solution)/shard_map/dot_general | solution.py:40
  343.4 3.5 convolution_convert_fusion.10
  347.0 3.0 fusion.101
  350.1 2.0 fusion.195
  352.1 12.9 %reduce-scatter.15.cloned.1.call-done = bf16[64,256]{1,0:T(8,128)(2,1)} async-done(((bf16[256,256]{1,0:T(8,128)(2,1)}), bf16[64,256]{1,0:T(8,128)(2,1)}) %reduce-scatter.15.cloned.1.call-update) | async-done | bytes 32784 | tf_op jit(solution)/shard_map/reduce_scatter | solution.py:232
  367.4 1.9 fusion.268
  369.3 13.6 %all_gather.15 = bf16[256,256]{1,0:T(8,128)(2,1)S(1)} all-gather(bf16[64,256]{1,0:T(8,128)(2,1)S(1)} %collective-permute-done.3), channel_id=1, replica_groups=mesh['groups'=2,'segment'=4,'head'=4] {'head'}, dimensions={0}, use_global_device_ids=true | all-gather | bytes 163840 | tf_op jit(solution)/shard_map/all_gather | solution.py:241
  383.5 2.3 convolution_convert_fusion
  385.8 5.4 %fusion.11 = (f32[8,256]{1,0:T(8,128)S(1)}, f32[8,256]{1,0:T(8,128)S(1)}, f32[256,256,8]{1,0,2:T(8,128)}) fusion(f32[8,256]{1,0:T(8,128)S(1)} %copy-done.68, f32[256,256,8]{1,0,2:T(8,128)} %get-tuple-element.76, pred[256,256]{0,1:T(8,128)(4,1)S(1)} %copy-done.30, f32[256,256,8]{1,0,2:T(8,128)} %fusion.101, bf16[256,2048]{1,0:T(8,128)(2,1)} %copy-done.20, ...), kind=kOutput, calls=%fused_computation.26 | convolution fusion | flops 272658432 | bytes 8478724 | tf_op jit(solution)/shard_map/iknd,jkd->knij/dot_general | solution.py:110
  391.2 4.0 convert_bitcast_fusion
  398.6 3.8 convolution_convert_fusion.3
  402.3 2.7 copy.77
  405.0 2.2 convolution_convert_fusion.6
  409.1 3.6 fusion.6
  412.7 2.9 convolution_add_fusion.1
  415.6 5.1 %multiply_reduce_fusion = (f32[256]{0:T(256)S(1)}, f32[256,2048]{1,0:T(8,128)}) fusion(f32[256,2048]{1,0:T(8,128)} %copy-done.2, f32[2048]{0:T(1024)S(1)} %bitcast.680, f32[256,2048]{1,0:T(8,128)} %convolution_add_fusion.1, bf16[1,2048,512]{2,1,0:T(8,128)(2,1)S(1)} %copy-done, s32[]{:T(128)S(6)} %select_n.142, bf16[256,8,128]{2,1,0:T(8,128)(2,1)} %bitcast.670, ...), kind=kOutput, calls=%fused_computation.43 | convolution fusion | flops 270565120 | bytes 8397828 | tf_op jit(solution)/shard_map/dot_general | solution.py:40
  420.7 3.5 convolution_convert_fusion.9
  428.0 17.6 %reduce-scatter.17.cloned.1.call-done = bf16[64,256]{1,0:T(8,128)(2,1)} async-done(((bf16[256,256]{1,0:T(8,128)(2,1)}), bf16[64,256]{1,0:T(8,128)(2,1)}) %reduce-scatter.17.cloned.1.call-update) | async-done | bytes 32784 | tf_op jit(solution)/shard_map/reduce_scatter | solution.py:232
  (250 shorter events, 69.3 us)
Async XLA Ops:
  7.2 108.5 %copy-start = (bf16[1,2048,512]{2,1,0:T(8,128)(2,1)S(1)}, bf16[1,2048,512]{2,1,0:T(8,128)(2,1)}, u32[]{:S(2)}) copy-start(bf16[1,2048,512]{2,1,0:T(8,128)(2,1)} %param.24) | copy-start | bytes 6291460
  7.2 133.1 %reduce-scatter.7.cloned.1.call-start = ((), (), s32[]{:S(2)}) async-start(), calls=%async_computation.6 | async-start | bytes 163840 | tf_op jit(solution)/shard_map/reduce_scatter | solution.py:211
  9.5 106.2 %copy-start.26 = (pred[256,256]{0,1:T(8,128)(4,1)}, pred[256,256]{0,1:T(8,128)(4,1)S(1)}, u32[]{:S(2)}) copy-start(pred[256,256]{0,1:T(8,128)(4,1)S(1)} %iota_compare_fusion) | copy-start | bytes 196612
  9.6 84.3 %copy-start.49 = (bf16[1,256,256]{2,1,0:T(8,128)(2,1)S(1)}, bf16[1,256,256]{2,1,0:T(8,128)(2,1)}, u32[]{:S(2)}) copy-start(bf16[1,256,256]{2,1,0:T(8,128)(2,1)} %param.15) | copy-start | bytes 393220
  13.6 81.3 %copy-start.1 = (bf16[1,256,2048]{2,1,0:T(8,128)(2,1)S(1)}, bf16[1,256,2048]{2,1,0:T(8,128)(2,1)}, u32[]{:S(2)}) copy-start(bf16[1,256,2048]{2,1,0:T(8,128)(2,1)} %param.19) | copy-start | bytes 3145732
  107.6 4.0 copy-start.40
  107.6 4.1 copy-start.77
  121.6 83.0 %reduce-scatter.9.cloned.1.call-start = ((), (), s32[]{:S(2)}) async-start(), calls=%async_computation.7 | async-start | bytes 163840 | tf_op jit(solution)/shard_map/reduce_scatter | solution.py:211
  141.8 4.4 collective-permute-start
  144.2 19.5 %copy-start.66 = (f32[256]{0:T(256)}, f32[256]{0:T(256)S(1)}, u32[]{:S(2)}) copy-start(f32[256]{0:T(256)S(1)} %get-tuple-element.33) | copy-start | bytes 3076
  163.7 4.1 copy-start.15
  164.4 5.7 %copy-start.12 = (bf16[256,2048]{1,0:T(8,128)(2,1)}, bf16[256,2048]{1,0:T(8,128)(2,1)S(1)}, u32[]{:S(2)}) copy-start(bf16[256,2048]{1,0:T(8,128)(2,1)S(1)} %get-tuple-element.19) | copy-start | bytes 3145732
  164.4 6.2 %copy-start.14 = (bf16[256,2048]{1,0:T(8,128)(2,1)}, bf16[256,2048]{1,0:T(8,128)(2,1)S(1)}, u32[]{:S(2)}) copy-start(bf16[256,2048]{1,0:T(8,128)(2,1)S(1)} %get-tuple-element.20) | copy-start | bytes 3145732
  164.4 8.6 %copy-start.13 = (bf16[256,2048]{1,0:T(8,128)(2,1)}, bf16[256,2048]{1,0:T(8,128)(2,1)S(1)}, u32[]{:S(2)}) copy-start(bf16[256,2048]{1,0:T(8,128)(2,1)S(1)} %get-tuple-element.21) | copy-start | bytes 3145732
  173.0 4.1 copy-start.27
  185.6 106.6 %reduce-scatter.13.cloned.1.call-start = ((), (), s32[]{:S(2)}) async-start(), calls=%async_computation.9 | async-start | bytes 163840 | tf_op jit(solution)/shard_map/reduce_scatter | solution.py:232
  185.7 5.0 %copy-start.71 = (f32[256]{0:T(256)S(1)}, f32[256]{0:T(256)}, u32[]{:S(2)}) copy-start(f32[256]{0:T(256)} %get-tuple-element.74) | copy-start | bytes 3076
  185.7 5.6 %copy-start.22 = (bf16[256,256]{1,0:T(8,128)(2,1)S(1)}, bf16[256,256]{1,0:T(8,128)(2,1)}, u32[]{:S(2)}) copy-start(bf16[256,256]{1,0:T(8,128)(2,1)} %copy-done.21) | copy-start | bytes 393220
  205.5 3.1 collective-permute-start.1
  208.5 23.6 %copy-start.10 = (f32[256,256,8]{1,0,2:T(8,128)}, f32[256,256,8]{1,0,2:T(8,128)S(1)}, u32[]{:S(2)}) copy-start(f32[256,256,8]{1,0,2:T(8,128)S(1)} %fusion.142) | copy-start | bytes 6291460
  208.6 15.2 %copy-start.23 = (bf16[256,256]{1,0:T(8,128)(2,1)S(1)}, bf16[256,256]{1,0:T(8,128)(2,1)}, u32[]{:S(2)}) copy-start(bf16[256,256]{1,0:T(8,128)(2,1)} %copy-done.21) | copy-start | bytes 393220
  225.9 3.7 copy-start.16
  227.3 3.6 copy-start.20
  230.9 4.5 copy-start.8
  231.5 3.9 copy-start.64
  232.1 3.3 copy-start.53
  235.4 5.0 %copy-start.69 = (f32[8,256]{1,0:T(8,128)}, f32[8,256]{1,0:T(8,128)S(1)}, u32[]{:S(2)}) copy-start(f32[8,256]{1,0:T(8,128)S(1)} %get-tuple-element.5) | copy-start | bytes 24580
  240.4 4.1 copy-start.6
  240.4 4.1 copy-start.25
  240.4 4.1 copy-start.48
  244.6 3.6 copy-start.17
  257.2 3.6 copy-start.42
  257.2 3.6 copy-start.60
  257.3 3.6 copy-start.76
  263.7 5.1 %copy-start.67 = (f32[256]{0:T(256)S(1)}, f32[256]{0:T(256)}, u32[]{:S(2)}) copy-start(f32[256]{0:T(256)} %copy-done.66) | copy-start | bytes 3076
  263.7 5.1 %copy-start.74 = (f32[256]{0:T(256)S(1)}, f32[256]{0:T(256)}, u32[]{:S(2)}) copy-start(f32[256]{0:T(256)} %get-tuple-element.32) | copy-start | bytes 3076
  268.8 3.6 copy-start.70
  272.3 40.3 %copy-start.29 = (pred[256,256]{0,1:T(8,128)(4,1)S(1)}, pred[256,256]{0,1:T(8,128)(4,1)}, u32[]{:S(2)}) copy-start(pred[256,256]{0,1:T(8,128)(4,1)} %copy-done.26) | copy-start | bytes 196612
  272.3 92.7 %reduce-scatter.15.cloned.1.call-start = ((), (), s32[]{:S(2)}) async-start(), calls=%async_computation.10 | async-start | bytes 163840 | tf_op jit(solution)/shard_map/reduce_scatter | solution.py:232
  293.1 24.5 %copy-start.51 = (bf16[64,256]{1,0:T(8,128)(2,1)}, bf16[64,256]{1,0:T(8,128)(2,1)S(1)}, u32[]{:S(2)}) copy-start(bf16[64,256]{1,0:T(8,128)(2,1)S(1)} %add_convert_fusion.2) | copy-start | bytes 98308
  293.1 3.1 collective-permute-start.2
  317.6 4.1 copy-start.5
  317.6 4.1 copy-start.24
  331.9 3.6 copy-start.43
  331.9 3.6 copy-start.58
  331.9 3.6 copy-start.75
  343.4 3.6 copy-start.45
  343.4 3.6 copy-start.56
  347.0 78.7 %reduce-scatter.11.cloned.1.call-start = ((), (), s32[]{:S(2)}) async-start(), calls=%async_computation.8 | async-start | bytes 163840 | tf_op jit(solution)/shard_map/reduce_scatter | solution.py:211
  350.1 35.7 %copy-start.30 = (pred[256,256]{0,1:T(8,128)(4,1)S(1)}, pred[256,256]{0,1:T(8,128)(4,1)}, u32[]{:S(2)}) copy-start(pred[256,256]{0,1:T(8,128)(4,1)} %copy-done.26) | copy-start | bytes 196612
  350.1 35.7 %copy-start.68 = (f32[8,256]{1,0:T(8,128)S(1)}, f32[8,256]{1,0:T(8,128)}, u32[]{:S(2)}) copy-start(f32[8,256]{1,0:T(8,128)} %get-tuple-element.4) | copy-start | bytes 24580
  365.9 25.3 %copy-start.52 = (bf16[64,256]{1,0:T(8,128)(2,1)}, bf16[64,256]{1,0:T(8,128)(2,1)S(1)}, u32[]{:S(2)}) copy-start(bf16[64,256]{1,0:T(8,128)(2,1)S(1)} %add_convert_fusion.1) | copy-start | bytes 98308
  365.9 3.4 collective-permute-start.3
  391.2 4.0 copy-start.9
  391.2 4.0 copy-start.35
  391.2 4.0 copy-start.54
  402.3 5.0 %copy-start.55 = (f32[256,8]{0,1:T(8,128)S(1)}, f32[256,8]{0,1:T(8,128)}, u32[]{:S(2)}) copy-start(f32[256,8]{0,1:T(8,128)} %get-tuple-element.13) | copy-start | bytes 24580
  407.2 38.3 %reduce-scatter.17.cloned.1.call-start = ((), (), s32[]{:S(2)}) async-start(), calls=%async_computation.11 | async-start | bytes 163840 | tf_op jit(solution)/shard_map/reduce_scatter | solution.py:232
  409.1 3.6 copy-start.36
  409.1 3.6 copy-start.41
  409.1 3.6 copy-start.73
  415.6 5.1 %copy-start.62 = (f32[256]{0:T(256)S(1)}, f32[256]{0:T(256)}, u32[]{:S(2)}) copy-start(f32[256]{0:T(256)} %copy-done.61) | copy-start | bytes 3076
  415.6 5.1 %copy-start.72 = (f32[256]{0:T(256)S(1)}, f32[256]{0:T(256)}, u32[]{:S(2)}) copy-start(f32[256]{0:T(256)} %get-tuple-element.24) | copy-start | bytes 3076
  420.7 3.5 copy-start.38
  (24 other events, 42.4 us)
Sparse Core Ops, SparseCore 0:
  121.7 18.5 reduce-scatter.6
  185.7 18.8 reduce-scatter.8
  272.5 19.7 reduce-scatter.12
  347.1 17.8 reduce-scatter.14
  407.3 18.2 reduce-scatter.10
  427.8 17.6 reduce-scatter.16
where the time goes:
time: 463 us; the launch traced here: 455 us
  matrix products  156 us (34%)
  blocking collectives  133 us (29%)
  waiting for transfers between devices  69 us (15%)
  other arithmetic  47.6 us (10%)
  local copies, waits for them, and re-layouts  27.8 us (6%)
  between operations  15.2 us (3%)
  starting transfers between devices  6.18 us (1%)
    psum x1, blocking collectives, shards(): embedded = lax.psum(picked, ('segment', 'head')).astype(jnp.bfloat16)  78 us
    dot_general x15, matrix products, narrow_back(): lax.dot_general(former, latter, (((1,), (1,)), ((), ())), preferred_eleme...  51.8 us
    reduce_scatter x3, waiting for transfers between devices, shards(): lax.psum_scatter(partial_back.astype(jnp.bfloat16), 'head', scatter_dimen...  46.7 us
    all_gather x2, blocking collectives, shards(): forward_recv = lax.all_gather(arrived, 'head', axis=0, tiled=True)  27.6 us
    all_gather x2, blocking collectives, shards(): backward_recv = lax.all_gather(arrived_back, 'head', axis=0, tiled=True)  27.1 us
    reduce_scatter x3, waiting for transfers between devices, shards(): lax.psum_scatter(partial_value.astype(jnp.bfloat16), 'head', scatter_dime...  21.6 us
    dot_general x6, matrix products, probabilities(): jnp.einsum('iknd,jkd->knij', grouped, k_hat, preferred_element_type=jnp.f...  15.6 us
    dot_general x3, matrix products, section_backward(): jnp.einsum('iknd,jkd->knij', grad_attended, values, preferred_element_typ...  15.3 us
  transfers between devices with their start and end apart: 10, of which 7 were waited for; matrix products, arithmetic and copies ran while one was open for 11% of the time, Pallas kernels for 0%

commit v1 on v0

--- a/solution.py
+++ b/solution.py
@@ -184,7 +184,11 @@
         jnp.float32
     )
     picked = jnp.where(inside[:, None], looked, 0.0)
-    embedded = lax.psum(picked, ("segment", "head")).astype(jnp.bfloat16)
+
+    def lay_pieces_all(row_data):
+        return jax.lax.psum(jax.lax.psum(row_data, "head"), "segment")
+
+    embedded = lay_pieces_all(picked).astype(jnp.bfloat16)
     tick_count = token_ids.shape[0]
     span_rows = token_ids.shape[1]
     embedded = embedded.reshape(tick_count, span_rows, -1)

time: 463 us -> 435 us (0.940)
  blocking collectives: 133 us -> 74.7 us
  waiting for transfers between devices: 69 us -> 107 us
    psum x1, blocking collectives: 78 us -> 20.3 us  [lay_pieces_all(): return jax.lax.psum(jax.lax.psum(row_data, 'head'), 'segment')]
    psum x0 -> x1, waiting for transfers between devices: none -> 29.6 us  [lay_pieces_all(): return jax.lax.psum(jax.lax.psum(row_data, 'head'), 'segment')]
    reduce_scatter x3, waiting for transfers between devices: 21.6 us -> 29.4 us  [shards(): lax.psum_scatter(partial_value.astype(jnp.bfloat16), 'head', scatter_dime...]
  transfers between devices with their start and end apart: 10 -> 11, of which waited for: 7 -> 9; matrix products, arithmetic and copies ran while one was open for 11% -> 14% of each run, Pallas kernels for 0% -> 0%
where the time goes in v1:
time: 435 us; the launch traced here: 427 us
  matrix products  154 us (35%)
  waiting for transfers between devices  107 us (25%)
  blocking collectives  74.7 us (17%)
  other arithmetic  45.2 us (10%)
  local copies, waits for them, and re-layouts  25.4 us (6%)
  between operations  15.2 us (3%)
  starting transfers between devices  5.63 us (1%)
    dot_general x15, matrix products, narrow_back(): lax.dot_general(former, latter, (((1,), (1,)), ((), ())), preferred_eleme...  50.9 us
    reduce_scatter x3, waiting for transfers between devices, shards(): lax.psum_scatter(partial_back.astype(jnp.bfloat16), 'head', scatter_dimen...  46.8 us
    psum x1, waiting for transfers between devices, lay_pieces_all(): return jax.lax.psum(jax.lax.psum(row_data, 'head'), 'segment')  29.6 us
    reduce_scatter x3, waiting for transfers between devices, shards(): lax.psum_scatter(partial_value.astype(jnp.bfloat16), 'head', scatter_dime...  29.4 us
    all_gather x2, blocking collectives, shards(): forward_recv = lax.all_gather(arrived, 'head', axis=0, tiled=True)  27.3 us
    all_gather x2, blocking collectives, shards(): backward_recv = lax.all_gather(arrived_back, 'head', axis=0, tiled=True)  27.1 us
    psum x1, blocking collectives, lay_pieces_all(): return jax.lax.psum(jax.lax.psum(row_data, 'head'), 'segment')  20.3 us
    dot_general x6, matrix products, probabilities(): jnp.einsum('iknd,jkd->knij', grouped, k_hat, preferred_element_type=jnp.f...  15.6 us
  transfers between devices with their start and end apart: 11, of which 9 were waited for; matrix products, arithmetic and copies ran while one was open for 14% of the time, Pallas kernels for 0%

profile of v1, /device:TPU:0, one launch (start us, length us, event | category | flops | bytes accessed | tf_op | source)
XLA Modules:
  0.0 426.6 jit_solution(5563716105099990430)
XLA Ops:
  9.5 3.2 gather_fusion
  14.1 3.8 fusion.32
  20.3 6.7 %copy.87 = bf16[1024,2048]{1,0:T(8,128)(2,1)} copy(bf16[1024,2048]{0,1:T(8,128)(2,1)} %bitcast.659) | data formatting | bytes 8388608 | tf_op jit(solution)/shard_map/dot_general | solution.py:57
  29.2 1.9 fusion.155
  31.2 29.6 %all-reduce.3.cloned.1.call-done = f32[768,256]{1,0:T(8,128)} async-done(((f32[768,256]{1,0:T(8,128)}), f32[768,256]{1,0:T(8,128)}) %all-reduce.3.cloned.1.call-update) | async-done | bytes 786448 | tf_op jit(solution)/shard_map/psum | solution.py:189
  60.8 20.3 %all-reduce.4 = bf16[768,256]{1,0:T(8,128)(2,1)} all-reduce(f32[768,256]{1,0:T(8,128)} %all-reduce.3.cloned.1.call-done), channel_id=1, replica_groups=mesh['groups'=2,'segment'=4,'head'=4] {'segment'}, use_global_device_ids=true, to_apply=%region_1.2 | all-reduce | flops 196608 | bytes 1179648 | tf_op jit(solution)/shard_map/psum | solution.py:189
  82.9 2.1 multiply_reduce_fusion.23
  86.7 1.9 fusion.23
  88.6 3.7 convolution_convert_fusion.5
  92.3 2.2 convolution_convert_fusion.8
  94.6 2.7 multiply_reduce_fusion.5
  98.3 14.7 %reduce-scatter.7.cloned.1.call-done = bf16[64,256]{1,0:T(8,128)(2,1)} async-done(((bf16[256,256]{1,0:T(8,128)(2,1)}), bf16[64,256]{1,0:T(8,128)(2,1)}) %reduce-scatter.7.cloned.1.call-update) | async-done | bytes 32784 | tf_op jit(solution)/shard_map/reduce_scatter | solution.py:215
  116.0 13.6 %all_gather.12 = bf16[256,256]{1,0:T(8,128)(2,1)S(1)} all-gather(bf16[64,256]{1,0:T(8,128)(2,1)S(1)} %collective-permute-done), channel_id=1, replica_groups=mesh['groups'=2,'segment'=4,'head'=4] {'head'}, dimensions={0}, use_global_device_ids=true | all-gather | bytes 163840 | tf_op jit(solution)/shard_map/all_gather | solution.py:224
  137.4 2.3 multiply_reduce_fusion.12
  142.7 2.9 multiply_reduce_fusion.14
  146.8 2.5 fusion.24
  149.3 3.8 convolution_convert_fusion.4
  153.1 2.2 convolution_convert_fusion.7
  157.3 3.1 fusion.141
  162.0 14.4 %reduce-scatter.9.cloned.1.call-done = bf16[64,256]{1,0:T(8,128)(2,1)} async-done(((bf16[256,256]{1,0:T(8,128)(2,1)}), bf16[64,256]{1,0:T(8,128)(2,1)}) %reduce-scatter.9.cloned.1.call-update) | async-done | bytes 32784 | tf_op jit(solution)/shard_map/reduce_scatter | solution.py:215
  178.5 1.8 fusion.142
  180.3 13.7 %all_gather.13 = bf16[256,256]{1,0:T(8,128)(2,1)S(1)} all-gather(bf16[64,256]{1,0:T(8,128)(2,1)S(1)} %collective-permute-done.1), channel_id=1, replica_groups=mesh['groups'=2,'segment'=4,'head'=4] {'head'}, dimensions={0}, use_global_device_ids=true | all-gather | bytes 163840 | tf_op jit(solution)/shard_map/all_gather | solution.py:224
  199.0 2.3 multiply_reduce_fusion.18
  203.9 3.3 fusion.31
  207.1 5.0 %fusion.19 = (f32[8,256]{1,0:T(8,128)}, f32[256,256,8]{1,0,2:T(8,128)}) fusion(f32[8,256]{1,0:T(8,128)S(1)} %get-tuple-element.5, f32[256,256,8]{1,0,2:T(8,128)} %fusion.141, pred[256,256]{0,1:T(8,128)(4,1)S(1)} %copy-done.30, bf16[256,2048]{1,0:T(8,128)(2,1)} %copy-done.14, bf16[1,2048,512]{2,1,0:T(8,128)(2,1)S(1)} %copy-done, s32[]{:T(128)S(6)} %select_n.142, ...), kind=kOutput, calls=%fused_computation.38 | convolution fusion | flops 271087616 | bytes 6373380 | tf_op jit(solution)/shard_map/iknd,jkd->knij/dot_general | solution.py:110
  212.1 4.1 convert_bitcast_fusion.2
  218.0 1.9 multiply_reduce_fusion.13
  219.9 2.8 multiply_reduce_fusion.15
  222.7 3.0 copy.65
  227.2 1.7 subtract_convert_fusion.8
  228.9 3.6 fusion.4
  232.5 2.9 convolution_add_fusion.5
  235.4 5.1 %multiply_reduce_fusion.4 = (f32[256]{0:T(256)S(1)}, f32[256,2048]{1,0:T(8,128)}) fusion(f32[256,2048]{1,0:T(8,128)} %get-tuple-element.49, f32[2048]{0:T(1024)S(1)} %bitcast.678, f32[256,2048]{1,0:T(8,128)} %convolution_add_fusion.5, bf16[1,2048,512]{2,1,0:T(8,128)(2,1)S(1)} %copy-done, s32[]{:T(128)S(6)} %select_n.142, ...), kind=kOutput, calls=%fused_computation.51 | convolution fusion | flops 270565120 | bytes 8397828 | tf_op jit(solution)/shard_map/dot_general | solution.py:40
  240.5 3.5 convolution_convert_fusion.11
  244.7 3.1 multiply_reduce_fusion.21
  247.7 16.2 %reduce-scatter.13.cloned.1.call-done = bf16[64,256]{1,0:T(8,128)(2,1)} async-done(((bf16[256,256]{1,0:T(8,128)(2,1)}), bf16[64,256]{1,0:T(8,128)(2,1)}) %reduce-scatter.13.cloned.1.call-update) | async-done | bytes 32784 | tf_op jit(solution)/shard_map/reduce_scatter | solution.py:236
  267.9 13.6 %all_gather.14 = bf16[256,256]{1,0:T(8,128)(2,1)S(1)} all-gather(bf16[64,256]{1,0:T(8,128)(2,1)S(1)} %collective-permute-done.2), channel_id=1, replica_groups=mesh['groups'=2,'segment'=4,'head'=4] {'head'}, dimensions={0}, use_global_device_ids=true | all-gather | bytes 163840 | tf_op jit(solution)/shard_map/all_gather | solution.py:245
  282.1 2.2 convolution_convert_fusion.1
  284.4 5.0 %fusion.15 = (f32[8,256]{1,0:T(8,128)}, f32[256,256,8]{1,0,2:T(8,128)}) fusion(f32[8,256]{1,0:T(8,128)} %get-tuple-element.6, f32[256,256,8]{1,0,2:T(8,128)} %copy-done.10, pred[256,256]{0,1:T(8,128)(4,1)S(1)} %copy-done.31, bf16[256,2048]{1,0:T(8,128)(2,1)} %copy-done.13, bf16[1,2048,512]{2,1,0:T(8,128)(2,1)S(1)} %copy-done, s32[]{:T(128)S(6)} %select_n.142, ...), kind=kOutput, calls=%fused_computation.32 | convolution fusion | flops 271087616 | bytes 6373380 | tf_op jit(solution)/shard_map/iknd,jkd->knij/dot_general | solution.py:110
  289.4 4.0 convert_bitcast_fusion.1
  295.1 1.9 multiply_reduce_fusion.11
  297.9 2.7 copy.71
  301.9 1.8 subtract_convert_fusion.7
  303.7 3.6 fusion.2
  307.3 2.9 convolution_add_fusion.3
  310.1 5.1 %multiply_reduce_fusion.2 = (f32[256]{0:T(256)S(1)}, f32[256,2048]{1,0:T(8,128)}) fusion(f32[256,2048]{1,0:T(8,128)} %copy-done.3, f32[2048]{0:T(1024)S(1)} %bitcast.679, f32[256,2048]{1,0:T(8,128)} %convolution_add_fusion.3, bf16[1,2048,512]{2,1,0:T(8,128)(2,1)S(1)} %copy-done, s32[]{:T(128)S(6)} %select_n.142, bf16[256,8,128]{2,1,0:T(8,128)(2,1)} %bitcast.671, ...), kind=kOutput, calls=%fused_computation.47 | convolution fusion | flops 270565120 | bytes 8397828 | tf_op jit(solution)/shard_map/dot_general | solution.py:40
  315.2 3.5 convolution_convert_fusion.10
  318.8 3.0 fusion.101
  321.9 2.0 fusion.195
  323.9 12.9 %reduce-scatter.15.cloned.1.call-done = bf16[64,256]{1,0:T(8,128)(2,1)} async-done(((bf16[256,256]{1,0:T(8,128)(2,1)}), bf16[64,256]{1,0:T(8,128)(2,1)}) %reduce-scatter.15.cloned.1.call-update) | async-done | bytes 32784 | tf_op jit(solution)/shard_map/reduce_scatter | solution.py:236
  339.1 1.9 fusion.268
  341.0 13.5 %all_gather.15 = bf16[256,256]{1,0:T(8,128)(2,1)S(1)} all-gather(bf16[64,256]{1,0:T(8,128)(2,1)S(1)} %collective-permute-done.3), channel_id=1, replica_groups=mesh['groups'=2,'segment'=4,'head'=4] {'head'}, dimensions={0}, use_global_device_ids=true | all-gather | bytes 163840 | tf_op jit(solution)/shard_map/all_gather | solution.py:245
  355.2 2.3 convolution_convert_fusion
  357.5 5.4 %fusion.11 = (f32[8,256]{1,0:T(8,128)S(1)}, f32[8,256]{1,0:T(8,128)S(1)}, f32[256,256,8]{1,0,2:T(8,128)}) fusion(f32[8,256]{1,0:T(8,128)S(1)} %copy-done.70, f32[256,256,8]{1,0,2:T(8,128)} %get-tuple-element.76, pred[256,256]{0,1:T(8,128)(4,1)S(1)} %copy-done.32, f32[256,256,8]{1,0,2:T(8,128)} %fusion.101, bf16[256,2048]{1,0:T(8,128)(2,1)} %copy-done.22, ...), kind=kOutput, calls=%fused_computation.26 | convolution fusion | flops 272658432 | bytes 8478724 | tf_op jit(solution)/shard_map/iknd,jkd->knij/dot_general | solution.py:110
  362.9 4.0 convert_bitcast_fusion
  370.3 3.8 convolution_convert_fusion.3
  374.1 2.7 copy.77
  376.7 2.2 convolution_convert_fusion.6
  379.0 1.8 subtract_convert_fusion.6
  380.8 3.6 fusion.6
  384.4 2.9 convolution_add_fusion.1
  387.3 5.1 %multiply_reduce_fusion = (f32[256]{0:T(256)S(1)}, f32[256,2048]{1,0:T(8,128)}) fusion(f32[256,2048]{1,0:T(8,128)} %copy-done.2, f32[2048]{0:T(1024)S(1)} %bitcast.680, f32[256,2048]{1,0:T(8,128)} %convolution_add_fusion.1, bf16[1,2048,512]{2,1,0:T(8,128)(2,1)S(1)} %copy-done, s32[]{:T(128)S(6)} %select_n.142, bf16[256,8,128]{2,1,0:T(8,128)(2,1)} %bitcast.670, ...), kind=kOutput, calls=%fused_computation.43 | convolution fusion | flops 270565120 | bytes 8397828 | tf_op jit(solution)/shard_map/dot_general | solution.py:40
  392.4 3.5 convolution_convert_fusion.9
  399.7 17.7 %reduce-scatter.17.cloned.1.call-done = bf16[64,256]{1,0:T(8,128)(2,1)} async-done(((bf16[256,256]{1,0:T(8,128)(2,1)}), bf16[64,256]{1,0:T(8,128)(2,1)}) %reduce-scatter.17.cloned.1.call-update) | async-done | bytes 32784 | tf_op jit(solution)/shard_map/reduce_scatter | solution.py:236
  (255 shorter events, 65.8 us)
Async XLA Ops:
  7.2 81.5 %copy-start = (bf16[1,2048,512]{2,1,0:T(8,128)(2,1)S(1)}, bf16[1,2048,512]{2,1,0:T(8,128)(2,1)}, u32[]{:S(2)}) copy-start(bf16[1,2048,512]{2,1,0:T(8,128)(2,1)} %param.24) | copy-start | bytes 6291460
  7.2 53.6 %all-reduce.3.cloned.1.call-start = ((), (), s32[]{:S(2)}) async-start(), calls=%async_computation.6 | async-start | bytes 1572864 | tf_op jit(solution)/shard_map/psum | solution.py:189
  14.0 99.0 %reduce-scatter.7.cloned.1.call-start = ((), (), s32[]{:S(2)}) async-start(), calls=%async_computation.7 | async-start | bytes 163840 | tf_op jit(solution)/shard_map/reduce_scatter | solution.py:215
  14.1 3.8 copy-start.46
  20.3 7.3 %copy-start.1 = (bf16[1,256,2048]{2,1,0:T(8,128)(2,1)S(1)}, bf16[1,256,2048]{2,1,0:T(8,128)(2,1)}, u32[]{:S(2)}) copy-start(bf16[1,256,2048]{2,1,0:T(8,128)(2,1)} %param.19) | copy-start | bytes 3145732
  82.9 3.8 copy-start.20
  94.6 81.8 %reduce-scatter.9.cloned.1.call-start = ((), (), s32[]{:S(2)}) async-start(), calls=%async_computation.8 | async-start | bytes 163840 | tf_op jit(solution)/shard_map/reduce_scatter | solution.py:215
  113.9 2.1 collective-permute-start
  115.8 17.6 %copy-start.68 = (f32[256]{0:T(256)}, f32[256]{0:T(256)S(1)}, u32[]{:S(2)}) copy-start(f32[256]{0:T(256)S(1)} %get-tuple-element.33) | copy-start | bytes 3076
  133.4 4.1 copy-start.17
  134.1 5.6 %copy-start.13 = (bf16[256,2048]{1,0:T(8,128)(2,1)}, bf16[256,2048]{1,0:T(8,128)(2,1)S(1)}, u32[]{:S(2)}) copy-start(bf16[256,2048]{1,0:T(8,128)(2,1)S(1)} %get-tuple-element.19) | copy-start | bytes 3145732
  134.1 6.2 %copy-start.15 = (bf16[256,2048]{1,0:T(8,128)(2,1)}, bf16[256,2048]{1,0:T(8,128)(2,1)S(1)}, u32[]{:S(2)}) copy-start(bf16[256,2048]{1,0:T(8,128)(2,1)S(1)} %get-tuple-element.20) | copy-start | bytes 3145732
  134.1 8.6 %copy-start.14 = (bf16[256,2048]{1,0:T(8,128)(2,1)}, bf16[256,2048]{1,0:T(8,128)(2,1)S(1)}, u32[]{:S(2)}) copy-start(bf16[256,2048]{1,0:T(8,128)(2,1)S(1)} %get-tuple-element.21) | copy-start | bytes 3145732
  142.7 4.1 copy-start.29
  155.3 108.6 %reduce-scatter.13.cloned.1.call-start = ((), (), s32[]{:S(2)}) async-start(), calls=%async_computation.10 | async-start | bytes 163840 | tf_op jit(solution)/shard_map/reduce_scatter | solution.py:236
  155.4 5.0 %copy-start.73 = (f32[256]{0:T(256)S(1)}, f32[256]{0:T(256)}, u32[]{:S(2)}) copy-start(f32[256]{0:T(256)} %get-tuple-element.74) | copy-start | bytes 3076
  155.4 5.6 %copy-start.24 = (bf16[256,256]{1,0:T(8,128)(2,1)S(1)}, bf16[256,256]{1,0:T(8,128)(2,1)}, u32[]{:S(2)}) copy-start(bf16[256,256]{1,0:T(8,128)(2,1)} %copy-done.23) | copy-start | bytes 393220
  177.2 3.1 copy-start.52
  177.2 3.1 collective-permute-start.1
  180.3 23.6 %copy-start.10 = (f32[256,256,8]{1,0,2:T(8,128)}, f32[256,256,8]{1,0,2:T(8,128)S(1)}, u32[]{:S(2)}) copy-start(f32[256,256,8]{1,0,2:T(8,128)S(1)} %fusion.142) | copy-start | bytes 6291460
  180.3 15.2 %copy-start.25 = (bf16[256,256]{1,0:T(8,128)(2,1)S(1)}, bf16[256,256]{1,0:T(8,128)(2,1)}, u32[]{:S(2)}) copy-start(bf16[256,256]{1,0:T(8,128)(2,1)} %copy-done.23) | copy-start | bytes 393220
  197.6 3.6 copy-start.18
  199.0 3.6 copy-start.22
  202.6 4.5 %copy-start.8 = (f32[256,8,128]{0,2,1:T(8,128)}, f32[256,8,128]{0,2,1:T(8,128)S(1)}, u32[]{:S(2)}) copy-start(f32[256,8,128]{0,2,1:T(8,128)S(1)} %get-tuple-element.65) | copy-start | bytes 3145732
  203.2 3.9 copy-start.66
  203.8 3.3 copy-start.55
  207.1 5.0 %copy-start.71 = (f32[8,256]{1,0:T(8,128)}, f32[8,256]{1,0:T(8,128)S(1)}, u32[]{:S(2)}) copy-start(f32[8,256]{1,0:T(8,128)S(1)} %get-tuple-element.5) | copy-start | bytes 24580
  212.1 4.1 copy-start.6
  212.1 4.1 copy-start.27
  212.1 4.1 copy-start.50
  216.3 3.6 copy-start.19
  228.9 3.6 copy-start.44
  228.9 3.6 copy-start.62
  228.9 3.6 copy-start.78
  235.4 5.1 %copy-start.69 = (f32[256]{0:T(256)S(1)}, f32[256]{0:T(256)}, u32[]{:S(2)}) copy-start(f32[256]{0:T(256)} %copy-done.68) | copy-start | bytes 3076
  235.4 5.1 %copy-start.76 = (f32[256]{0:T(256)S(1)}, f32[256]{0:T(256)}, u32[]{:S(2)}) copy-start(f32[256]{0:T(256)} %get-tuple-element.32) | copy-start | bytes 3076
  240.5 3.6 copy-start.72
  244.0 40.4 %copy-start.31 = (pred[256,256]{0,1:T(8,128)(4,1)S(1)}, pred[256,256]{0,1:T(8,128)(4,1)}, u32[]{:S(2)}) copy-start(pred[256,256]{0,1:T(8,128)(4,1)} %iota_compare_fusion) | copy-start | bytes 196612
  244.0 92.8 %reduce-scatter.15.cloned.1.call-start = ((), (), s32[]{:S(2)}) async-start(), calls=%async_computation.11 | async-start | bytes 163840 | tf_op jit(solution)/shard_map/reduce_scatter | solution.py:236
  264.8 24.6 %copy-start.53 = (bf16[64,256]{1,0:T(8,128)(2,1)}, bf16[64,256]{1,0:T(8,128)(2,1)S(1)}, u32[]{:S(2)}) copy-start(bf16[64,256]{1,0:T(8,128)(2,1)S(1)} %add_convert_fusion.2) | copy-start | bytes 98308
  264.8 3.1 collective-permute-start.2
  289.4 4.0 copy-start.5
  289.4 4.0 copy-start.26
  303.6 3.6 copy-start.45
  303.6 3.6 copy-start.60
  303.7 3.6 copy-start.77
  315.2 3.6 copy-start.47
  315.2 3.6 copy-start.58
  318.8 78.7 %reduce-scatter.11.cloned.1.call-start = ((), (), s32[]{:S(2)}) async-start(), calls=%async_computation.9 | async-start | bytes 163840 | tf_op jit(solution)/shard_map/reduce_scatter | solution.py:215
  321.9 35.6 %copy-start.32 = (pred[256,256]{0,1:T(8,128)(4,1)S(1)}, pred[256,256]{0,1:T(8,128)(4,1)}, u32[]{:S(2)}) copy-start(pred[256,256]{0,1:T(8,128)(4,1)} %iota_compare_fusion) | copy-start | bytes 196612
  321.9 35.6 %copy-start.70 = (f32[8,256]{1,0:T(8,128)S(1)}, f32[8,256]{1,0:T(8,128)}, u32[]{:S(2)}) copy-start(f32[8,256]{1,0:T(8,128)} %get-tuple-element.4) | copy-start | bytes 24580
  337.6 25.2 %copy-start.54 = (bf16[64,256]{1,0:T(8,128)(2,1)}, bf16[64,256]{1,0:T(8,128)(2,1)S(1)}, u32[]{:S(2)}) copy-start(bf16[64,256]{1,0:T(8,128)(2,1)S(1)} %add_convert_fusion.1) | copy-start | bytes 98308
  337.7 3.4 collective-permute-start.3
  362.9 4.0 copy-start.9
  362.9 4.0 copy-start.38
  362.9 4.0 copy-start.56
  374.1 5.0 %copy-start.57 = (f32[256,8]{0,1:T(8,128)S(1)}, f32[256,8]{0,1:T(8,128)}, u32[]{:S(2)}) copy-start(f32[256,8]{0,1:T(8,128)} %get-tuple-element.13) | copy-start | bytes 24580
  379.0 38.4 %reduce-scatter.17.cloned.1.call-start = ((), (), s32[]{:S(2)}) async-start(), calls=%async_computation.12 | async-start | bytes 163840 | tf_op jit(solution)/shard_map/reduce_scatter | solution.py:236
  380.8 3.6 copy-start.39
  380.8 3.6 copy-start.43
  380.8 3.6 copy-start.75
  387.3 5.1 %copy-start.64 = (f32[256]{0:T(256)S(1)}, f32[256]{0:T(256)}, u32[]{:S(2)}) copy-start(f32[256]{0:T(256)} %copy-done.63) | copy-start | bytes 3076
  387.3 5.1 %copy-start.74 = (f32[256]{0:T(256)S(1)}, f32[256]{0:T(256)}, u32[]{:S(2)}) copy-start(f32[256]{0:T(256)} %get-tuple-element.24) | copy-start | bytes 3076
  392.4 3.5 copy-start.41
  (26 other events, 43.9 us)
Sparse Core Ops, SparseCore 0:
  14.1 46.6 all-reduce.2
  94.7 18.3 reduce-scatter.6
  155.4 20.8 reduce-scatter.8
  244.1 19.7 reduce-scatter.12
  318.9 17.8 reduce-scatter.14
  379.1 18.3 reduce-scatter.10
  399.7 17.6 reduce-scatter.16
